TPU v7x, 256 devices: a whole 4x4x8 slice. The times are simulated.
256 devices in a mesh: cls: 8 (over x, core), ori: 32 (over z, y).
Axes of the slice: x: 4, y: 4, z: 8, core: 2. Of those that a mesh axis runs over, the one named last changes fastest.
Arguments:
- images: bfloat16 [2048, 20480], P('ori'), may hold values from -6 to 6
- projections: bfloat16 [8, 4608, 20480], P('cls', 'ori'), may hold values from -0.0390625 to 0.0390625
- log_prior: float32 [8, 4608], P('cls', 'ori'), may hold values from -4 to 300
- significant: int32 [2048, 4], P('ori'), may hold values from 0 to 31, all different within a row; in each aligned block of 64 rows (0 to 63, 64 to 127, ...) at most 12 rows name the same one
- shell_index: int32 [20480], replicated, may hold values from 0 to 99
- noise_inv: float32 [100], replicated, may hold values from 0.5 to 4
Outputs:
- class_sums: bfloat16 [8, 4608, 20480], P('cls', None, 'ori')
- log_evidence: float32 [2048], P('ori')
Inputs may be any that keep to these rules, and one draw needn't show every extreme that they name: `significant`: each row names 4 different blocks. Among the rows of one index of ori no block is named more than 12 times, and some block is named exactly 12 times.
All inputs are finite; a program needn't handle non-finite values.
Results may differ from a plain program's by a relative error of at most 0.0076.
Values may be sent and summed in bfloat16 or wider, within the bound.
A program may use at most 128 MiB of HBM per device.

v0:
```python
import jax
import jax.numpy as jnp
from jax import lax
from jax.experimental import pallas as pl
from jax.experimental.pallas import tpu as pltpu
from jax.sharding import PartitionSpec as P

MESH = pl.DeviceIdType.MESH
SENTINEL = -1e30
TILE = 128
NY = 4
NZ = 8
NX = 4


def mod(value, size):
    return lax.rem(value + size, size)


class Ring:
    def __init__(self, buf, view, pos, sizes, devs, send_sem, recv_sem):
        self.buf, self.view, self.pos, self.sizes, self.devs = buf, view, pos, sizes, devs
        self.send_sem, self.recv_sem = send_sem, recv_sem
        self.started = []
        nf = sizes[0]
        offsets = [0]
        for r in range(1, nf // 2):
            offsets += [-r, r]
        offsets.append(nf // 2)
        self.offsets = offsets

    def copy(self, ident, df, dg, n, r, d, ring):
        (f, g), (nf, ng) = self.pos, self.sizes
        half = d if r == n // 2 - 1 else None
        ref = self.view(self.buf, mod(f + df, nf), mod(g + dg, ng), half)
        return pltpu.make_async_remote_copy(
            src_ref=ref,
            dst_ref=ref,
            send_sem=self.send_sem.at[ident],
            recv_sem=self.recv_sem.at[ident],
            device_id=self.devs[ring](1 - 2 * d),
            device_id_type=MESH,
        )

    def send(self, *what):
        self.copy(*what).start()
        self.started.append(what)

    def f_what(self, r, d, hop):
        return (2 * r + d, -(1 - 2 * d) * (r + hop), 0, self.sizes[0], r, d, 0)

    def g_what(self, j, r, d, hop):
        nf, ng = self.sizes
        return (nf + (j * (ng // 2) + r) * 2 + d, self.offsets[j], -(1 - 2 * d) * (r + hop), ng, r, d, 1)

    def start(self):
        for d in (0, 1):
            self.send(*self.f_what(0, d, 0))
            self.send(*self.g_what(0, 0, d, 0))

    def f_rounds(self):
        return self.sizes[0] // 2

    def f_round(self, r):
        nf = self.sizes[0]
        for d in (0, 1):
            self.copy(*self.f_what(r, d, 1)).wait_recv()
            if r + 1 < nf // 2:
                self.send(*self.f_what(r + 1, d, 0))
        for j in (2 * r + 1, 2 * r + 2):
            if j < nf:
                for d in (0, 1):
                    self.send(*self.g_what(j, 0, d, 0))

    def g_step(self, i):
        nf, ng = self.sizes
        r, j = i // nf, i % nf
        for d in (0, 1):
            self.copy(*self.g_what(j, r, d, 1)).wait_recv()
            if r + 1 < ng // 2:
                self.send(*self.g_what(j, r + 1, d, 0))

    def finish(self):
        for what in self.started:
            self.copy(*what).wait_send()


def lines_of(top, full):
    row = lax.broadcasted_iota(jnp.int32, (8, TILE), 0)
    out = jnp.zeros((8, TILE), jnp.float32)
    at = 0
    for value in (top, full):
        for t in range(value.shape[1] // TILE):
            out = jnp.where(row == at, value[:, t * TILE : (t + 1) * TILE], out)
            at += 1
    return out


def step_kernel(
    img_ref,
    proj_ref,
    prior_ref,
    listed_ref,
    shell_ref,
    noise_ref,
    shared,
    packed,
    evidence_ref,
    evidence,
    weights,
    images,
    proj,
    norms,
    received,
    part,
    from_pair,
    summed,
    from_far,
    stat,
    spread,
    band,
    ranks,
    tops,
    share,
    own_sem,
    proj_send,
    proj_recv,
    img_send,
    img_recv,
    post_send,
    post_recv,
    pair_send,
    pair_recv,
    far_send,
    far_recv,
    stat_send,
    stat_recv,
    spread_send,
    spread_recv,
    band_send,
    band_recv,
):
    cls = lax.axis_index("cls")
    ori = lax.axis_index("ori")
    x, core = cls // 2, cls % 2
    z, y = ori // NY, ori % NY
    classes = 2 * NX
    owners = NY * NZ
    img_rows = images.shape[2]
    width = proj.shape[2]
    col = band.shape[3]
    slots = received.shape[0]
    orients = proj.shape[1]
    cap = slots // owners
    tiles = slots // TILE

    def slot_of(k):
        return (k % 2) * NX + k // 2

    def peer(d, sign):
        c = (core + d) % 2
        return mod(x + sign * (d // 2), NX) * 2 + c

    def cls_dev(k):
        return (k, ori)

    def y_dev(step):
        return (cls, z * NY + mod(y + step, NY))

    def z_dev(step):
        return (cls, mod(z + step, NZ) * NY + y)

    barrier = pltpu.get_barrier_semaphore()
    greeted = [cls_dev(peer(d, 1)) for d in range(1, classes)]
    greeted += [y_dev(d) for d in range(1, NY)]
    greeted += [z_dev(d) for d in range(1, NZ)]
    for dev in greeted:
        pl.semaphore_signal(barrier, inc=1, device_id=dev, device_id_type=MESH)
    own_img = pltpu.make_async_copy(
        img_ref.at[:, pl.ds(pl.multiple_of(cls * width, TILE), width)], received.at[0:img_rows], own_sem.at[0]
    )
    own_img.start()
    own_proj = pltpu.make_async_copy(
        proj_ref.at[:, pl.ds(pl.multiple_of(cls * width, TILE), width)], proj.at[slot_of(cls)], own_sem.at[1]
    )
    own_proj.start()
    shells = shell_ref[...]
    level = jnp.zeros(shells.shape, jnp.float32)
    for j in range(noise_ref.shape[0]):
        level = jnp.where(shells == j, noise_ref[j], level)
    weights[...] = level
    named = jnp.zeros((owners, img_rows), jnp.bool_)
    block_row = lax.broadcasted_iota(jnp.int32, (owners, img_rows), 0)
    for j in range(listed_ref.shape[0]):
        named = jnp.logical_or(named, listed_ref[j : j + 1, :] == block_row)
    named = jnp.where(named, 1.0, 0.0).astype(jnp.bfloat16)
    image_row = lax.broadcasted_iota(jnp.int32, (img_rows, TILE), 0)
    image_lane = lax.broadcasted_iota(jnp.int32, (img_rows, TILE), 1) % img_rows
    twice = jnp.where(image_row == image_lane, 1.0, 0.0).astype(jnp.bfloat16)
    before = jnp.where(image_row < image_lane, 1.0, 0.0).astype(jnp.bfloat16)
    there = jnp.dot(named, twice, preferred_element_type=jnp.float32)
    rank = jnp.dot(named, before, preferred_element_type=jnp.float32)
    rank = jnp.where(there > 0.5, rank, -1.0)
    rank = jnp.concatenate([rank, jnp.zeros((img_rows - owners, TILE), jnp.float32)], axis=0)
    images[z, y, :, width : width + TILE] = rank.astype(jnp.bfloat16)

    def weight_row(j):
        return weights[pl.ds(cls * (width // TILE) + j, 1), :]

    pl.semaphore_wait(barrier, len(greeted))

    def proj_copy(d, to, frm):
        return pltpu.make_async_remote_copy(
            src_ref=proj_ref.at[:, pl.ds(pl.multiple_of(to * width, TILE), width)],
            dst_ref=proj.at[slot_of(frm)],
            send_sem=proj_send.at[d],
            recv_sem=proj_recv.at[d],
            device_id=cls_dev(to),
            device_id_type=MESH,
        )

    for d in (2, 3, 6, 7, 4, 5, 1):
        proj_copy(d, peer(d, 1), cls).start()
    own_img.wait()
    for j in range(width // TILE):
        lane = slice(j * TILE, (j + 1) * TILE)
        images[z, y, :, lane] = (received[0:img_rows, lane].astype(jnp.float32) * weight_row(j)).astype(jnp.bfloat16)

    def slice_view(swap):
        def view(buf, fi, gi, half):
            zi, yi = (fi, gi) if swap else (gi, fi)
            n = buf.shape[2]
            if half is None:
                return buf.at[zi, yi]
            return buf.at[zi, yi, pl.ds(half * (n // 2), n // 2)]

        return view

    def gather(buf, send_sem, recv_sem, f_hooks, g_hooks):
        rings = (
            Ring(buf, slice_view(False), (y, z), (NY, NZ), (y_dev, z_dev), send_sem, recv_sem),
            Ring(buf, slice_view(True), (z, y), (NZ, NY), (z_dev, y_dev), send_sem, recv_sem),
        )

        def both(act):
            for c in range(2):

                @pl.when(core == c)
                def _():
                    act(rings[c])

        both(lambda ring: ring.start())
        for r in range(NZ // 2):
            both(lambda ring: ring.f_round(r) if r < ring.f_rounds() else None)
            for hook in f_hooks.get(r, ()):
                hook()
        for i in range(NY * NZ // 2):
            both(lambda ring: ring.g_step(i))
            for hook in g_hooks.get(i, ()):
                hook()
        both(lambda ring: ring.finish())

    def norm_of(d):
        def run():
            if d == 0:
                own_proj.wait()
            else:
                proj_copy(d, peer(d, 1), peer(d, -1)).wait_recv()
            at = slot_of(peer(d, -1)) if d else slot_of(cls)
            norm = jnp.zeros((orients, TILE), jnp.float32)
            for j in range(width // TILE):
                lane = slice(j * TILE, (j + 1) * TILE)
                wide = proj[at, :, lane].astype(jnp.float32)
                norm = norm + wide * wide * weight_row(j)
            norms[at] = 0.5 * jnp.sum(norm, axis=1, keepdims=True)

        return run

    order = (0, 1, 2, 3, 6, 7)
    gather(images, img_send, img_recv, {}, {10 + i: [norm_of(d)] for i, d in enumerate(order)})

    owner_x, owner_core = z // 2, z % 2
    role = mod(x - owner_x, NX)
    on_line = core == owner_core
    half = NZ // 2
    band_cols = pl.ds(pl.multiple_of(y * col, TILE), col)
    ahead = (mod(x + 1, NX) * 2 + core, ori)
    behind = (mod(x - 1, NX) * 2 + core, ori)
    pair = (x * 2 + 1 - core, ori)
    is_owner = jnp.logical_and(on_line, role == 0)

    def band_copy(j, lane, first):
        return pltpu.make_async_remote_copy(
            src_ref=images.at[j, :, :, band_cols] if first else band.at[j],
            dst_ref=band.at[j],
            send_sem=band_send.at[lane, j],
            recv_sem=band_recv.at[j],
            device_id=(ahead, behind, pair)[lane],
            device_id_type=MESH,
        )

    own_band = pltpu.make_async_copy(images.at[:, :, :, band_cols], band, own_sem.at[2])

    def band_first(js):
        @pl.when(is_owner)
        def _():
            for j in js:
                band_copy(j, 0, True).start()
                band_copy(half + j, 1, True).start()
            for j in js:
                band_copy(j, 2, True).start()
                band_copy(half + j, 2, True).start()

    def relay_plan(s):
        near, mid, far = s - 1, s - 2, s - 3
        plan = {1: [], 2: [], 3: []}
        if 0 <= near < half:
            plan[1].append((near, 0))
            plan[3].append((half + near, 1))
        if 0 <= mid < half:
            plan[2] += [(mid, 0), (half + mid, 1)]
        if 0 <= far < half:
            plan[1].append((half + far, None))
            plan[3].append((far, None))
        return plan

    def band_step(s):
        def run():
            for k, todo in relay_plan(s).items():

                @pl.when(jnp.logical_and(on_line, role == k))
                def _():
                    for j, lane in todo:
                        band_copy(j, 2, False).wait_recv()
                        if lane is not None:
                            band_copy(j, lane, False).start()
                        band_copy(j, 2, False).start()

        return run

    def nth_piece(n):
        return jnp.where(
            role == 3, (n + half) % NZ, jnp.where(role == 2, (n % 2) * half + n // 2, n)
        )

    def band_sent():
        @pl.when(is_owner)
        def _():
            for j in range(half):
                band_copy(j, 0, True).wait_send()
                band_copy(half + j, 1, True).wait_send()
            for j in range(NZ):
                band_copy(j, 2, True).wait_send()

        for k in (1, 2, 3):

            @pl.when(jnp.logical_and(on_line, role == k))
            def _():
                for s in range(1, half + 3):
                    for j, lane in relay_plan(s)[k]:
                        if lane is not None:
                            band_copy(j, lane, False).wait_send()
                        band_copy(j, 2, False).wait_send()

    @pl.when(is_owner)
    def _():
        own_band.start()

    band_first((0, 1))

    lanes = NY * img_rows
    lane_src = lax.broadcasted_iota(jnp.int32, (NY * cap, lanes), 1) // img_rows
    row_id = lax.broadcasted_iota(jnp.int32, (NY * cap, lanes), 0)
    place = jnp.where(lane_src == row_id // cap, (row_id % cap).astype(jnp.float32), -2.0)
    o_row = lax.broadcasted_iota(jnp.int32, (owners, TILE), 0) == ori
    low = lax.broadcasted_iota(jnp.int32, (owners, TILE), 1) < img_rows

    def pick_rows(zi, carry):
        tables = [
            images[zi, yi, 0:owners, width : width + TILE].astype(jnp.float32) for yi in range(NY)
        ]
        both = [jnp.where(low, tables[0], tables[1]), jnp.where(low, tables[2], tables[3])]
        for h in range(2):
            ranks[zi, :, h * TILE : (h + 1) * TILE] = both[h]
        line = jnp.concatenate(
            [jnp.sum(jnp.where(o_row, both[h], 0.0), axis=0, keepdims=True) for h in range(2)], axis=1
        )
        pick = jnp.where(place == line, 1.0, 0.0).astype(jnp.bfloat16)
        data = images[zi, :, :, 0:width].reshape(lanes, width)
        found = jnp.dot(pick, data, preferred_element_type=jnp.float32)
        received[pl.ds(pl.multiple_of(zi * NY * cap, 16), NY * cap), :] = found.astype(jnp.bfloat16)
        return carry

    lax.fori_loop(0, NZ, pick_rows, 0)
    for d in range(1, classes):
        if d not in order:
            norm_of(d)()

    def pair_copy(j):
        return pltpu.make_async_remote_copy(
            src_ref=part.at[j],
            dst_ref=from_pair.at[j],
            send_sem=pair_send.at[j],
            recv_sem=pair_recv.at[j],
            device_id=pair,
            device_id_type=MESH,
        )

    def far_copy(dx):
        return pltpu.make_async_remote_copy(
            src_ref=summed.at[mod(x + dx, NX)],
            dst_ref=from_far.at[dx],
            send_sem=far_send.at[dx],
            recv_sem=far_recv.at[dx],
            device_id=(mod(x + dx, NX) * 2 + core, ori),
            device_id_type=MESH,
        )

    def partial(c):
        block = proj[pl.ds(c * NX, NX)].reshape(NX * orients, width)
        score = lax.dot_general(block, received[...], (((1,), (1,)), ((), ())), preferred_element_type=jnp.float32)
        return score.reshape(NX, orients, slots) - norms[pl.ds(c * NX, NX)]

    part[...] = partial(1 - core)
    for j in range(NX):
        pair_copy(j).start()
    summed[...] = partial(core)
    for dx in (2, 1, 3):
        j = mod(x + dx, NX)
        pair_copy(j).wait_recv()
        summed[j] = summed[j] + from_pair[j]
        far_copy(dx).start()
    band_step(1)()
    band_first((2, 3))
    pair_copy(x).wait_recv()
    square = (orients, orients)
    diagonal = lax.broadcasted_iota(jnp.int32, square, 0) == lax.broadcasted_iota(jnp.int32, square, 1)
    prior = jnp.sum(jnp.where(diagonal, jnp.broadcast_to(prior_ref[...], square), 0.0), axis=1, keepdims=True)
    total = summed[x] + from_pair[x] + prior
    for dx in range(1, NX):
        far_copy(dx).wait_recv()
        total = total + from_far[dx]
    score = total
    peak = jnp.max(score, axis=0, keepdims=True)
    amount = jnp.sum(jnp.exp(score - peak), axis=0, keepdims=True)
    stat[cls] = lines_of(peak, amount)

    def stat_copy(d, frm):
        return pltpu.make_async_remote_copy(
            src_ref=stat.at[frm],
            dst_ref=stat.at[frm],
            send_sem=stat_send.at[d],
            recv_sem=stat_recv.at[d],
            device_id=cls_dev(peer(d, 1)),
            device_id_type=MESH,
        )

    for d in range(1, classes):
        stat_copy(d, cls).start()
    for d in range(1, classes):
        stat_copy(d, peer(d, -1)).wait_recv()
    top = []
    full = []
    for t in range(tiles):
        best = stat[0, t : t + 1]
        for k in range(1, classes):
            best = jnp.maximum(best, stat[k, t : t + 1])
        whole = jnp.zeros_like(best)
        for k in range(classes):
            whole = whole + stat[k, tiles + t : tiles + t + 1] * jnp.exp(stat[k, t : t + 1] - best)
        top.append(best)
        full.append(whole)
    top = jnp.concatenate(top, axis=1)
    full = jnp.concatenate(full, axis=1)
    spread[z, y] = lines_of(top, full)

    def spread_y(d, yi):
        return pltpu.make_async_remote_copy(
            src_ref=spread.at[z, yi],
            dst_ref=spread.at[z, yi],
            send_sem=spread_send.at[d],
            recv_sem=spread_recv.at[d],
            device_id=y_dev(d),
            device_id_type=MESH,
        )

    def spread_z(d, zi):
        return pltpu.make_async_remote_copy(
            src_ref=spread.at[zi],
            dst_ref=spread.at[zi],
            send_sem=spread_send.at[NY + d],
            recv_sem=spread_recv.at[NY + d],
            device_id=z_dev(d),
            device_id_type=MESH,
        )

    for d in range(1, NY):
        spread_y(d, y).start()
    shared[z, y] = jnp.exp(score - top).astype(jnp.bfloat16)

    def spread_on():
        for d in range(1, NY):
            spread_y(d, mod(y - d, NY)).wait_recv()
        for d in range(1, NZ):
            spread_z(d, z).start()

    def spread_end():
        for d in range(1, NZ):
            spread_z(d, mod(z - d, NZ)).wait_recv()
        for zi in range(NZ):
            for yi in range(NY):
                o = zi * NY + yi
                for t in range(2 * tiles):
                    tops[t, o : o + 1, :] = spread[zi, yi, t : t + 1, :]

    def shares_of(qs):
        def run():
            lanes_of = {q: slice((q % 2) * TILE, (q % 2 + 1) * TILE) for q in qs}
            rank = {q: ranks[q // 2, :, lanes_of[q]].astype(jnp.int32) for q in qs}
            named = {q: rank[q] >= 0 for q in qs}
            spot = {
                q: jnp.maximum(rank[q], 0) + jnp.where(low, 2 * q * cap, (2 * q + 1) * cap) for q in qs
            }

            def look(q, base):
                first, last = 2 * q * cap // TILE, (2 * (q + 1) * cap - 1) // TILE
                found = None
                for t in range(first, last + 1):
                    local = spot[q] - t * TILE
                    value = jnp.take_along_axis(tops[base + t], jnp.clip(local, 0, TILE - 1), axis=1)
                    found = value if found is None else jnp.where(local >= 0, value, found)
                return found

            highs = {q: jnp.where(named[q], look(q, 0), SENTINEL) for q in qs}
            wholes = {q: jnp.where(named[q], look(q, tiles), 0.0) for q in qs}
            best = {q: jnp.max(highs[q], axis=0, keepdims=True) for q in qs}
            raised = {q: jnp.where(named[q], jnp.exp(highs[q] - best[q]), 0.0) for q in qs}
            whole = {q: jnp.sum(raised[q] * wholes[q], axis=0, keepdims=True) for q in qs}
            part_of = {q: raised[q] / whole[q] for q in qs}
            for q in qs:
                share[q // 2, :, lanes_of[q]] = part_of[q]
                evidence[q : q + 1, :] = best[q] + jnp.log(whole[q])

        return run

    def pack(n):
        def run():
            g = nth_piece(n)

            @pl.when(jnp.logical_not(on_line))
            def _():
                band_copy(g, 2, False).wait_recv()

            data = band[g].reshape(lanes, col)
            blocks = 8

            def some(b, carry):
                first = pl.multiple_of(b * blocks, blocks)
                table = ranks[g, pl.ds(first, blocks), :]
                factor = share[g, pl.ds(first, blocks), :]
                picks = [
                    jnp.where(place == table[i : i + 1], factor[i : i + 1], 0.0).astype(jnp.bfloat16)
                    for i in range(blocks)
                ]
                found = jnp.dot(
                    jnp.concatenate(picks, axis=0), data, preferred_element_type=jnp.float32
                ).astype(jnp.bfloat16)
                packed[pl.ds(first, blocks), pl.ds(pl.multiple_of(g * NY * cap, 16), NY * cap), :] = found.reshape(
                    blocks, NY * cap, col
                )
                return carry

            lax.fori_loop(0, owners // blocks, some, 0)

        return run

    def quarter(n):
        return shares_of(range(n * 4, n * 4 + 4))

    hooks = {
        0: [spread_end],
        1: [band_step(3), quarter(0)],
        2: [quarter(1)],
        3: [quarter(2)],
        4: [band_step(4), quarter(3)],
        5: [pack(0)],
        6: [pack(1)],
        7: [band_step(5), pack(2)],
        8: [pack(3)],
        9: [pack(4)],
        10: [band_step(6), pack(5)],
        11: [pack(6)],
        12: [pack(7)],
    }

    @pl.when(is_owner)
    def _():
        own_band.wait()

    gather(shared, post_send, post_recv, {0: [spread_on, band_step(2)]}, hooks)

    line = evidence[pl.ds(ori // 2, 1), :]
    other = pltpu.roll(line, img_rows, 1)
    evidence_ref[...] = jnp.where(ori % 2 == 0, line, other)[:, 0:img_rows]
    band_sent()
    for d in range(1, classes):
        proj_copy(d, peer(d, 1), cls).wait_send()
        stat_copy(d, cls).wait_send()
    for j in range(NX):
        pair_copy(j).wait_send()
        if j:
            far_copy(j).wait_send()
    for d in range(1, NY):
        spread_y(d, y).wait_send()
    for d in range(1, NZ):
        spread_z(d, z).wait_send()


def step(images, projection, prior, listed, shells, noise, slots, col):
    img_rows, freqs = images.shape
    orients = projection.shape[0]
    width = freqs // (2 * NX)
    wide = width + TILE
    owners = NY * NZ
    dma = pltpu.SemaphoreType.DMA
    classes = 2 * NX
    messages = NZ + NZ * NY
    block = (NX, orients, slots)
    vmem = pl.BlockSpec(memory_space=pltpu.VMEM)
    bf16, f32 = jnp.bfloat16, jnp.float32
    return pl.pallas_call(
        step_kernel,
        out_shape=(
            jax.ShapeDtypeStruct((NZ, NY, orients, slots), bf16),
            jax.ShapeDtypeStruct((owners, slots, col), bf16),
            jax.ShapeDtypeStruct((1, img_rows), f32),
        ),
        in_specs=[
            pl.BlockSpec(memory_space=pltpu.HBM),
            pl.BlockSpec(memory_space=pltpu.HBM),
            vmem,
            vmem,
            vmem,
            pl.BlockSpec(memory_space=pltpu.SMEM),
        ],
        out_specs=(vmem, vmem, vmem),
        scratch_shapes=[
            pltpu.VMEM((owners // 2, TILE), f32),
            pltpu.VMEM(shells.shape, f32),
            pltpu.VMEM((NZ, NY, img_rows, wide), bf16),
            pltpu.VMEM((classes, orients, width), bf16),
            pltpu.VMEM((classes, orients, 1), f32),
            pltpu.VMEM((slots, width), bf16),
            pltpu.VMEM(block, f32),
            pltpu.VMEM(block, f32),
            pltpu.VMEM(block, f32),
            pltpu.VMEM(block, f32),
            pltpu.VMEM((classes, 8, TILE), f32),
            pltpu.VMEM((NZ, NY, 8, TILE), f32),
            pltpu.VMEM((NZ, NY, img_rows, col), bf16),
            pltpu.VMEM((NZ, owners, 2 * TILE), f32),
            pltpu.VMEM((8, owners, TILE), f32),
            pltpu.VMEM((NZ, owners, 2 * TILE), f32),
            dma((3,)),
            dma((classes,)),
            dma((classes,)),
            dma((messages,)),
            dma((messages,)),
            dma((messages,)),
            dma((messages,)),
            dma((NX,)),
            dma((NX,)),
            dma((NX,)),
            dma((NX,)),
            dma((classes,)),
            dma((classes,)),
            dma((NY + NZ,)),
            dma((NY + NZ,)),
            dma((3, NZ)),
            dma((NZ,)),
        ],
        compiler_params=pltpu.CompilerParams(
            collective_id=0, has_side_effects=True, vmem_limit_bytes=28 * 1024 * 1024
        ),
        name="estep",
    )(images, projection, prior, listed, shells, noise)


def sums_kernel(shared, packed, out_ref, stage, out_sem):
    owners = packed.shape[0]
    orients = shared.shape[2]

    def out_copy(o, s):
        return pltpu.make_async_copy(
            stage.at[s], out_ref.at[pl.ds(pl.multiple_of(o * orients, 16), orients), :], out_sem.at[s]
        )

    depth = stage.shape[0] // 2

    def emit(t, carry):
        base = lax.rem(t, 2) * depth

        @pl.when(t > 1)
        def _():
            for s in range(depth):
                out_copy((t - 2) * depth + s, base + s).wait()

        for s in range(depth):
            o = t * depth + s
            stage[base + s] = jnp.dot(
                shared[o // NY, o % NY], packed[o], preferred_element_type=jnp.float32
            ).astype(jnp.bfloat16)
        for s in range(depth):
            out_copy(t * depth + s, base + s).start()
        return carry

    rounds = owners // depth
    lax.fori_loop(0, rounds, emit, 0)
    for t in (rounds - 2, rounds - 1):
        for s in range(depth):
            out_copy(t * depth + s, (t % 2) * depth + s).wait()


def sums(shared, packed):
    owners, slots, col = packed.shape
    orients = shared.shape[2]
    vmem = pl.BlockSpec(memory_space=pltpu.VMEM)
    return pl.pallas_call(
        sums_kernel,
        out_shape=jax.ShapeDtypeStruct((owners * orients, col), jnp.bfloat16),
        in_specs=[vmem, vmem],
        out_specs=pl.BlockSpec(memory_space=pltpu.HBM),
        scratch_shapes=[pltpu.VMEM((8, orients, col), jnp.bfloat16), pltpu.SemaphoreType.DMA((8,))],
        compiler_params=pltpu.CompilerParams(vmem_limit_bytes=8 * 1024 * 1024),
        name="sums",
    )(shared, packed)


def body(images, projections, log_prior, significant, shell_index, noise_inv):
    owners = lax.axis_size("ori")
    rows, width = images.shape
    listed = significant.shape[1]
    cap = max(2, 3 * rows * listed // (2 * owners))
    shared, packed, evidence = step(
        pltpu.with_memory_space_constraint(images, pltpu.HBM),
        pltpu.with_memory_space_constraint(projections[0], pltpu.HBM),
        log_prior,
        significant.T,
        shell_index.reshape(width // TILE, TILE),
        noise_inv,
        owners * cap,
        width // owners,
    )
    return (sums(shared, packed)[None], evidence[0])


def solution(mesh):
    in_specs = (P("ori", None), P("cls", "ori", None), P("cls", "ori"), P("ori", None), P(), P())
    out_specs = (P("cls", None, "ori"), P("ori"))
    return jax.shard_map(body, mesh=mesh, in_specs=in_specs, out_specs=out_specs, check_vma=False)
```

profile of v0, /device:TPU:3, one launch (start us, length us, event | category | flops | bytes accessed | tf_op | source)
XLA Modules:
  0.0 151.6 jit_solution(2235069597192837493)
XLA Ops:
  0.6 0.0 copy-start
  0.6 0.9 copy-done
  1.5 0.0 copy-start.1
  1.5 0.7 copy-done.1
  2.2 0.0 copy-start.2
  2.2 0.7 copy-done.2
  2.9 0.0 copy-start.3
  2.9 0.7 copy-done.3
  3.5 140.9 %estep.1 = (bf16[8,4,144,384]{3,2,1,0:T(8,128)(2,1)S(1)}, bf16[32,384,640]{2,1,0:T(8,128)(2,1)S(1)}, f32[1,64]{1,0:T(1,128)S(1)}) custom-call(bf16[64,20480]{1,0:T(8,128)(2,1)} %img_ref.1, bf16[144,20480]{1,0:T(8,128)(2,1)} %bitcast.8, f32[1,144]{1,0:T(1,128)S(1)} %copy-done.2, s32[4,64]{1,0:T(4,128)S(1)} %bitcast.6, s32[160,128]{1,0:T(8,128)S(1)} %bitcast.5, ...), custom_call_target="tpu_custom_call" | custom-call | tf_op jit(solution)/shard_map/estep/pallas_call | solution.py:631
  144.5 6.6 %sums.1 = bf16[4608,640]{1,0:T(8,128)(2,1)} custom-call(bf16[8,4,144,384]{3,2,1,0:T(8,128)(2,1)S(1)} %get-tuple-element.5.shared, bf16[32,384,640]{2,1,0:T(8,128)(2,1)S(1)} %get-tuple-element.6.packed), custom_call_target="tpu_custom_call" | custom-call | tf_op jit(solution)/shard_map/sums/pallas_call | solution.py:728
  151.1 0.5 copy.9
Async XLA Ops:
  0.6 0.9 copy-start
  1.5 0.7 copy-start.1
  2.2 0.7 copy-start.2
  2.9 0.7 copy-start.3
where the time goes:
time: 155 us; the launch traced here: 152 us
  Pallas kernels  148 us (95%)
  local copies, waits for them, and re-layouts  3.41 us (2%)
    pallas_call x1, Pallas kernels, step(): pl.pallas_call(step_kernel, out_shape=(jax.ShapeDtypeStruct((NZ, NY, orie...  141 us
    pallas_call x1, Pallas kernels, sums(): pl.pallas_call(sums_kernel, out_shape=jax.ShapeDtypeStruct((owners * orie...  6.63 us
    unnamed x9, local copies, waits for them, and re-layouts  3.41 us

commit v1 on v0

--- a/solution.py
+++ b/solution.py
@@ -99,13 +99,16 @@
 def step_kernel(
     img_ref,
     proj_ref,
-    prior_ref,
-    listed_ref,
-    shell_ref,
+    prior_in,
+    listed_in,
+    shell_in,
     noise_ref,
     shared,
     packed,
     evidence_ref,
+    prior_ref,
+    listed_ref,
+    shell_ref,
     evidence,
     weights,
     images,
@@ -170,6 +173,12 @@
     def z_dev(step):
         return (cls, mod(z + step, NZ) * NY + y)
 
+    small = [
+        pltpu.make_async_copy(src, dst, own_sem.at[3 + i])
+        for i, (src, dst) in enumerate(((shell_in, shell_ref), (listed_in, listed_ref), (prior_in, prior_ref)))
+    ]
+    for cp in small:
+        cp.start()
     barrier = pltpu.get_barrier_semaphore()
     greeted = [cls_dev(peer(d, 1)) for d in range(1, classes)]
     greeted += [y_dev(d) for d in range(1, NY)]
@@ -184,6 +193,8 @@
         proj_ref.at[:, pl.ds(pl.multiple_of(cls * width, TILE), width)], proj.at[slot_of(cls)], own_sem.at[1]
     )
     own_proj.start()
+    for cp in small:
+        cp.wait()
     shells = shell_ref[...]
     level = jnp.zeros(shells.shape, jnp.float32)
     for j in range(noise_ref.shape[0]):
@@ -638,13 +649,16 @@
         in_specs=[
             pl.BlockSpec(memory_space=pltpu.HBM),
             pl.BlockSpec(memory_space=pltpu.HBM),
-            vmem,
-            vmem,
-            vmem,
+            pl.BlockSpec(memory_space=pltpu.HBM),
+            pl.BlockSpec(memory_space=pltpu.HBM),
+            pl.BlockSpec(memory_space=pltpu.HBM),
             pl.BlockSpec(memory_space=pltpu.SMEM),
         ],
         out_specs=(vmem, vmem, vmem),
         scratch_shapes=[
+            pltpu.VMEM(prior.shape, f32),
+            pltpu.VMEM(listed.shape, jnp.int32),
+            pltpu.VMEM(shells.shape, jnp.int32),
             pltpu.VMEM((owners // 2, TILE), f32),
             pltpu.VMEM(shells.shape, f32),
             pltpu.VMEM((NZ, NY, img_rows, wide), bf16),
@@ -661,7 +675,7 @@
             pltpu.VMEM((NZ, owners, 2 * TILE), f32),
             pltpu.VMEM((8, owners, TILE), f32),
             pltpu.VMEM((NZ, owners, 2 * TILE), f32),
-            dma((3,)),
+            dma((6,)),
             dma((classes,)),
             dma((classes,)),
             dma((messages,)),
@@ -744,10 +758,10 @@
     shared, packed, evidence = step(
         pltpu.with_memory_space_constraint(images, pltpu.HBM),
         pltpu.with_memory_space_constraint(projections[0], pltpu.HBM),
-        log_prior,
-        significant.T,
-        shell_index.reshape(width // TILE, TILE),
-        noise_inv,
+        pltpu.with_memory_space_constraint(log_prior, pltpu.HBM),
+        pltpu.with_memory_space_constraint(significant.T, pltpu.HBM),
+        pltpu.with_memory_space_constraint(shell_index.reshape(width // TILE, TILE), pltpu.HBM),
+        pltpu.with_memory_space_constraint(noise_inv, pltpu.HBM),
         owners * cap,
         width // owners,
     )

time: 155 us -> 152 us (0.981)
  local copies, waits for them, and re-layouts: 3.41 us -> 0.51 us
    unnamed x9 -> x1, local copies, waits for them, and re-layouts: 3.41 us -> 0.51 us
where the time goes in v1:
time: 152 us; the launch traced here: 149 us
  Pallas kernels  148 us (97%)
    pallas_call x1, Pallas kernels, step(): pl.pallas_call(step_kernel, out_shape=(jax.ShapeDtypeStruct((NZ, NY, orie...  141 us
    pallas_call x1, Pallas kernels, sums(): pl.pallas_call(sums_kernel, out_shape=jax.ShapeDtypeStruct((owners * orie...  6.64 us

profile of v1, /device:TPU:3, one launch (start us, length us, event | category | flops | bytes accessed | tf_op | source)
XLA Modules:
  0.0 149.1 jit_solution(3611193390377999133)
XLA Ops:
  0.6 141.3 %estep.1 = (bf16[8,4,144,384]{3,2,1,0:T(8,128)(2,1)S(1)}, bf16[32,384,640]{2,1,0:T(8,128)(2,1)S(1)}, f32[1,64]{1,0:T(1,128)S(1)}) custom-call(bf16[64,20480]{1,0:T(8,128)(2,1)} %img_ref.1, bf16[144,20480]{1,0:T(8,128)(2,1)} %bitcast.6, f32[1,144]{1,0:T(1,128)} %prior_in.1, s32[4,64]{1,0:T(4,128)} %bitcast.9, s32[160,128]{1,0:T(8,128)} %bitcast.8, f32[100]{0:T(128)} %noise_ref.1), custom_call_target="tpu_custom_call" | custom-call | tf_op jit(solution)/shard_map/estep/pallas_call | solution.py:642
  141.9 6.6 %sums.1 = bf16[4608,640]{1,0:T(8,128)(2,1)} custom-call(bf16[8,4,144,384]{3,2,1,0:T(8,128)(2,1)S(1)} %get-tuple-element.5.shared, bf16[32,384,640]{2,1,0:T(8,128)(2,1)S(1)} %get-tuple-element.6.packed), custom_call_target="tpu_custom_call" | custom-call | tf_op jit(solution)/shard_map/sums/pallas_call | solution.py:742
  148.6 0.5 copy.9

commit v2 on v1

--- a/solution.py
+++ b/solution.py
@@ -590,25 +590,26 @@
 
     hooks = {
         0: [spread_end],
-        1: [band_step(3), quarter(0)],
+        1: [quarter(0)],
         2: [quarter(1)],
-        3: [quarter(2)],
-        4: [band_step(4), quarter(3)],
+        3: [band_step(3), quarter(2)],
+        4: [quarter(3)],
         5: [pack(0)],
-        6: [pack(1)],
-        7: [band_step(5), pack(2)],
+        6: [band_step(4), pack(1)],
+        7: [pack(2)],
         8: [pack(3)],
-        9: [pack(4)],
-        10: [band_step(6), pack(5)],
+        9: [band_step(5), pack(4)],
+        10: [pack(5)],
         11: [pack(6)],
-        12: [pack(7)],
+        12: [band_step(6)],
+        13: [pack(7)],
     }
 
     @pl.when(is_owner)
     def _():
         own_band.wait()
 
-    gather(shared, post_send, post_recv, {0: [spread_on, band_step(2)]}, hooks)
+    gather(shared, post_send, post_recv, {0: [spread_on], 1: [band_step(2)]}, hooks)
 
     line = evidence[pl.ds(ori // 2, 1), :]
     other = pltpu.roll(line, img_rows, 1)

time: 152 us -> 151 us (level); the launches traced: 149 us -> 151 us
  Pallas kernels: 148 us -> 150 us
    pallas_call x1, Pallas kernels: 141 us -> 143 us  [step(): pl.pallas_call(step_kernel, out_shape=(jax.ShapeDtypeStruct((NZ, NY, orie...]
where the time goes in v2:
time: 151 us
  Pallas kernels  150 us (99%)
    pallas_call x1, Pallas kernels, step(): pl.pallas_call(step_kernel, out_shape=(jax.ShapeDtypeStruct((NZ, NY, orie...  143 us
    pallas_call x1, Pallas kernels, sums(): pl.pallas_call(sums_kernel, out_shape=jax.ShapeDtypeStruct((owners * orie...  6.64 us

profile of v2, /device:TPU:3, one launch (start us, length us, event | category | flops | bytes accessed | tf_op | source)
XLA Modules:
  0.0 151.0 jit_solution(1637461187987597367)
XLA Ops:
  0.6 143.2 %estep.1 = (bf16[8,4,144,384]{3,2,1,0:T(8,128)(2,1)S(1)}, bf16[32,384,640]{2,1,0:T(8,128)(2,1)S(1)}, f32[1,64]{1,0:T(1,128)S(1)}) custom-call(bf16[64,20480]{1,0:T(8,128)(2,1)} %img_ref.1, bf16[144,20480]{1,0:T(8,128)(2,1)} %bitcast.6, f32[1,144]{1,0:T(1,128)} %prior_in.1, s32[4,64]{1,0:T(4,128)} %bitcast.9, s32[160,128]{1,0:T(8,128)} %bitcast.8, f32[100]{0:T(128)} %noise_ref.1), custom_call_target="tpu_custom_call" | custom-call | tf_op jit(solution)/shard_map/estep/pallas_call | solution.py:643
  143.8 6.6 %sums.1 = bf16[4608,640]{1,0:T(8,128)(2,1)} custom-call(bf16[8,4,144,384]{3,2,1,0:T(8,128)(2,1)S(1)} %get-tuple-element.5.shared, bf16[32,384,640]{2,1,0:T(8,128)(2,1)S(1)} %get-tuple-element.6.packed), custom_call_target="tpu_custom_call" | custom-call | tf_op jit(solution)/shard_map/sums/pallas_call | solution.py:743
  150.5 0.5 copy.9
